TPU v7x, 32 devices: a whole 2x2x4 slice. The times are simulated.
32 devices in a mesh: tm: 8 (over z, y), tensor: 4 (over x, core).
Axes of the slice: x: 2, y: 2, z: 4, core: 2. Of those that a mesh axis runs over, the one named last changes fastest.
Arguments:
- frames_in: bfloat16 [8, 1024, 768], P('tm'), may hold values from -16 to 16
- norm_gain: float32 [768], replicated, may hold values from 0.1 to 1.9
- w_qkv: bfloat16 [768, 3, 768], P(None, None, 'tensor'), may hold values from -0.21650635 to 0.21650635
- w_out: bfloat16 [768, 768], P('tensor'), may hold values from -0.21875 to 0.21875
- keep_runs: int32 [8, 16, 2], replicated, may hold values from 0 to 1023, as said below
- out_cotangent: bfloat16 [8, 1024, 768], P('tm'), may hold values from -6 to 6
Outputs:
- block_out: bfloat16 [8, 1024, 768], P('tm', None, 'tensor')
- grad_in: bfloat16 [8, 1024, 768], P('tm', None, 'tensor')
- grad_qkv: bfloat16 [768, 3, 768], P('tm', None, 'tensor')
- grad_proj: bfloat16 [768, 768], P('tensor', 'tm')
- grad_gain: float32 [768], P('tensor')
Inputs may be any that keep to these rules, and one draw needn't show every extreme that they name: keep_runs[t, r] = (first, length) is the r-th run of kept positions of frame t; the 16 runs of a frame are disjoint, in rising order, and lie within the frame's 1024 positions.
All inputs are finite; a program needn't handle non-finite values.
Results may differ from a plain program's by a relative error of at most 0.034.
Values may be sent and summed in bfloat16 or wider, within the bound.
No kernel may reach another device: no remote copies, remote signals or barrier semaphores. Data moves between devices by JAX's collectives and lax.ppermute only.
A program may use at most 128 MiB of HBM per device.

v0:
```python
import functools

import jax
import jax.numpy as jnp
from jax import lax
from jax.experimental import pallas as pl
from jax.experimental.pallas import tpu as pltpu
from jax.sharding import PartitionSpec as P

D = 768
H = 12
HEAD = D // H
LANES = 128
EPS = 1e-05
MASKED = -1000000000.0

BF = jnp.bfloat16
F32 = jnp.float32
VMEM_LIMIT = 12 * 1024 * 1024
WHOLE_VMEM = 61*1024*1024


def exchange(value, axis, bit):
    size = lax.axis_size(axis)
    return lax.ppermute(value, axis, [(i, i ^ bit) for i in range(size)])


def dot(a, b):
    return lax.dot_general(a, b, (((1,), (0,)), ((), ())), preferred_element_type=F32)


def dot_t(a, b):
    return lax.dot_general(a, b, (((1,), (1,)), ((), ())), preferred_element_type=F32)


def t_dot(a, b):
    return lax.dot_general(a, b, (((0,), (0,)), ((), ())), preferred_element_type=F32)


def standardize(x):
    x = x.astype(F32)
    shifted = x - jnp.mean(x, axis=-1, keepdims=True)
    inverse = lax.rsqrt(jnp.mean(shifted * shifted, axis=-1, keepdims=True) + EPS)
    return shifted * inverse, inverse


def block_rows(value, frames, b, rows):
    q = value.shape[0] // frames
    if q == rows:
        return value
    cut = value.reshape(frames, q, value.shape[1])[:, b * rows : (b + 1) * rows]
    return cut.reshape(frames * rows, value.shape[1])


def split_heads(value):
    lane = lax.broadcasted_iota(jnp.int32, value.shape, 1)
    zero = jnp.zeros_like(value)
    return jnp.concatenate(
        [jnp.where(lane < HEAD, value, zero), jnp.where(lane >= HEAD, value, zero)], axis=0
    )


def join_heads(value):
    n = value.shape[0] // 2
    lane = lax.broadcasted_iota(jnp.int32, (n, value.shape[1]), 1)
    return jnp.where(lane < HEAD, value[:n], value[n:])


def put_rows(ref, b, rows, col, value):
    ref[:, b * rows : (b + 1) * rows, col : col + value.shape[1]] = value.reshape(
        ref.shape[0], rows, value.shape[1]
    )


def all_rows(parts):
    return jnp.concatenate(list(parts), axis=0)


def halves(value, who):
    half = value.shape[-1] // 2
    low, high = value[..., :half], value[..., half:]
    first = who[0] // 2 == 0
    return jnp.where(first, low, high), jnp.where(first, high, low)


def own_and_other(value, who):
    share = value.shape[-1] // 2
    low, high = value[..., :share], value[..., share:]
    first = who[0] % 2 == 0
    return jnp.where(first, low, high), jnp.where(first, high, low)


def two_parts(value):
    top = value.astype(BF).astype(F32)
    return top, value - top


def copy_all(pairs, sems):
    copies = [pltpu.make_async_copy(src, dst, sems.at[i]) for i, (src, dst) in enumerate(pairs)]
    for copy in copies:
        copy.start()
    for copy in copies:
        copy.wait()


def send_x_kernel(j, x_in, x_out, sems):
    copy_all([(x_in.at[i, j[0]], x_out.at[i]) for i in range(x_out.shape[0])], sems)


def send_c_kernel(n_near, n_slots, k, j, c_in, *refs):
    outs, sems = refs[:n_slots], refs[n_slots]
    pairs = []
    for s in range(n_slots):
        if s < n_near:
            for g in range(2):
                pairs.append((c_in.at[k[0] ^ s, j[0] ^ (2 * g)], outs[s].at[g]))
        else:
            pairs.append((c_in.at[k[0] ^ s, j[0]], outs[s]))
    copy_all(pairs, sems)


def stack_kernel(*refs):
    parts, out = refs[:-1], refs[-1]
    for i, ref in enumerate(parts):
        out[i] = ref[...]


def kept_row(runs, frames, rows, first):
    lane = lax.broadcasted_iota(jnp.int32, (frames, frames * rows), 1)
    frame = lax.broadcasted_iota(jnp.int32, (frames, frames * rows), 0)
    place = first + lane % rows
    begins, lengths = runs[:, 0, :], runs[:, 1, :]
    hits = jnp.zeros((frames, frames * rows), F32)
    for r in range(begins.shape[1]):
        begin = begins[:, r : r + 1]
        here = (place >= begin) & (place < begin + lengths[:, r : r + 1])
        hits = jnp.where(here, 1.0, hits)
    return jnp.sum(jnp.where(frame == lane // rows, hits, 0.0), axis=0, keepdims=True)


def attend_kernel(
    frames, rows, picks, n_te, g, who, where, gain_in, wa, wb, oa, ob, runs, x_in, *refs
):
    c_in, rest = refs[: len(picks)], refs[len(picks) :]
    c_all, normed, mixed, pcot, keep, send, stats, gains = rest
    if len(picks) == 1:
        c_all[...] = c_in[0][...]
    else:
        for s, (ref, pick) in enumerate(zip(c_in, picks)):
            c_all[where[0] ^ s] = ref[...] if pick is None else ref[pick]
    gain = gain_in[...].reshape(1, x_in.shape[2])
    wq, wk, wv = (all_rows((wa[i], wb[i])) for i in range(3))
    wout = all_rows((oa[...], ob[...]))
    width, full = wout.shape
    chunk = x_in.shape[1]
    tokens = frames * chunk
    n_rows = frames * rows
    standard, _ = standardize(x_in[...].reshape(tokens, full))
    n = (standard * gain).astype(BF)
    normed[...] = n
    qs, ks, vs = (dot_t(n, w).astype(BF) for w in (wq, wk, wv))
    c = c_all[...].reshape(tokens, full)
    mc = dot_t(c, wout).astype(BF)
    row = lax.broadcasted_iota(jnp.int32, (n_rows, n_rows), 0)
    col = lax.broadcasted_iota(jnp.int32, (n_rows, n_rows), 1)
    first = (where[0] * n_te + (who[0] ^ (2 * g))) * chunk
    for b in range(chunk // rows):
        across = kept_row(runs, frames, rows, first + b * rows)
        down = jnp.sum(jnp.where(row == col, across, 0.0), axis=1, keepdims=True)
        inside = jnp.where(row % rows == col % rows, across * down, 0.0)
        for p in range(width // LANES):
            cols = slice(p * LANES, (p + 1) * LANES)
            q, k, v, dm = (block_rows(z[:, cols], frames, b, rows) for z in (qs, ks, vs, mc))
            kk, vv = split_heads(k), split_heads(v)
            s = dot_t(q, kk) * HEAD ** (-0.5)
            dw = dot_t(dm, vv).astype(BF).astype(F32)
            w_parts, d_parts = [], []
            for e in range(2):
                part = jnp.where(inside > 0, s[:, e * n_rows : (e + 1) * n_rows], MASKED)
                top = jnp.max(part, axis=-1, keepdims=True)
                ex = jnp.exp(part - top) * inside
                total = jnp.sum(ex, axis=-1, keepdims=True)
                we = ex / jnp.where(total > 0, total, 1.0)
                de = dw[:, e * n_rows : (e + 1) * n_rows]
                inner = jnp.sum(we * de, axis=-1, keepdims=True)
                w_parts.append(we.astype(BF))
                d_parts.append((we * (de - inner) * HEAD ** (-0.5)).astype(BF))
            w = jnp.concatenate(w_parts, axis=1)
            ds = jnp.concatenate(d_parts, axis=1)
            put_rows(mixed, b, rows, p * LANES, dot(w, vv).astype(BF))
            put_rows(pcot, b, rows, p * LANES, dot(ds, kk).astype(BF))
            put_rows(pcot, b, rows, width + p * LANES, join_heads(t_dot(ds, q)).astype(BF))
            put_rows(pcot, b, rows, 2 * width + p * LANES, join_heads(t_dot(w, dm)).astype(BF))
    y = dot(mixed[...].reshape(tokens, width), wout)
    mine, other = halves(y, who)
    keep[0] = mine
    send[:tokens] = other.astype(BF)
    pc = pcot[...].reshape(tokens, 3 * width)
    nc = dot(pc, all_rows((wq, wk, wv)))
    nn = n.astype(F32) * nc
    mean_plain = jnp.sum(nc * gain, axis=-1, keepdims=True)
    mean_cross = jnp.sum(nn, axis=-1, keepdims=True)
    total_gain = jnp.sum(nn, axis=0, keepdims=True) / gain
    lane = lax.broadcasted_iota(jnp.int32, (tokens, LANES), 1)
    both = (jnp.where(lane == 0, mean_plain, mean_cross) * (1.0 / full)).T[:2]
    half = full // 2
    stats[...] = both
    mine, other = halves(nc, who)
    keep[1] = mine
    send[tokens : 2 * tokens] = other.astype(BF)
    mine, other = halves(total_gain, who)
    gains[...] = mine
    if half > tokens:
        both = jnp.concatenate([both, jnp.zeros((2, half - tokens), F32)], axis=1)
    sent = []
    for value in (both[:1], both[1:], other):
        sent += two_parts(value)
    send[2 * tokens :] = stacked_rows(sent, 16, half).astype(BF)


def stacked_rows(values, count, lanes):
    at = lax.broadcasted_iota(jnp.int32, (count, lanes), 0)
    block = jnp.zeros((count, lanes), F32)
    for i, value in enumerate(values):
        block = jnp.where(at == i, value, block)
    return block


def local_kernel(source, out):
    out[...] = source[...]


def grads_kernel(own, n0, n1, p0, p1, c0, c1, m0, m1, out):
    width = m0.shape[1]
    share = width // 2
    columns = []
    for which in range(4):
        if which < 3:
            left, right, base = (n0, n1), (p0, p1), which * width
        else:
            left, right, base = (c0, c1), (m0, m1), 0
        cols = slice(base, base + width)
        value = t_dot(left[0][...], right[0][:, cols]) + t_dot(left[1][...], right[1][:, cols])
        columns.append(value[:, :share] if own else value[:, share:])
    out[...] = jnp.concatenate(columns, axis=1).astype(out.dtype)


def halve_kernel(n_blocks, orders, step, n_held, where, *refs):
    held, moved, outs = refs[:n_held], refs[n_held : 2 * n_held], refs[2 * n_held :]
    k = where[0]
    for i, order in enumerate(orders):
        column = outs[2 * i].shape[-1]
        cols = slice(i * column, (i + 1) * column) if n_held == 1 else slice(None)
        keep, send = outs[2 * i : 2 * i + 2]
        source, came = held[i % n_held], moved[i % n_held]
        left = [bit for bit in (1 << b for b in range(n_blocks.bit_length())) if bit < n_blocks]
        left = [bit for bit in left if bit not in order[:step]]
        here = left.index(order[step])
        mine = (k // order[step]) % 2
        for n in range(keep.shape[0]):
            low = n % (1 << here)
            base = ((n >> here) << (here + 1)) + low
            stay = base + (mine << here)
            leave = base + ((1 - mine) << here)
            keep[n] = source[stay, :, cols] + came[stay, :, cols].astype(F32)
            send[n] = (source[leave, :, cols] + came[leave, :, cols].astype(F32)).astype(BF)


def last_grads_kernel(held_a, held_b, moved_a, moved_b, qkv, proj):
    share = proj.shape[0]
    a = held_a[0] + moved_a[0].astype(F32)
    b = held_b[0] + moved_b[0].astype(F32)
    qkv[0] = a[:, :share].astype(BF)
    qkv[1] = a[:, share:].astype(BF)
    qkv[2] = b[:, :share].astype(BF)
    proj[...] = b[:, share:].T.astype(BF)


def finish_kernel(who, x_in, c_in, gain_in, keep, recv, stats, *refs):
    tokens = keep.shape[1]
    full = x_in.shape[-1]
    own, swap = refs[:2] if len(refs) == 2 else refs[3:5]
    x = x_in[...].reshape(tokens, full)
    standard, inverse = standardize(x)
    sent = recv[2 * tokens :].astype(F32)
    plain = stats[:1] + sent[0:1, :tokens] + sent[1:2, :tokens]
    cross = stats[1:2] + sent[2:3, :tokens] + sent[3:4, :tokens]
    both = stacked_rows((plain, cross), 8, tokens).T
    mean_plain, mean_cross = both[:, 0:1], both[:, 1:2]
    out = halves(x.astype(F32), who)[0] + keep[0] + recv[:tokens].astype(F32)
    scaled = keep[1] + recv[tokens : 2 * tokens].astype(F32)
    scaled = scaled * halves(gain_in[...].reshape(1, full), who)[0]
    through = inverse * (scaled - mean_plain - halves(standard, who)[0] * mean_cross)
    back = halves(c_in[...].reshape(tokens, full).astype(F32), who)[0] + through
    for i, value in enumerate((out, back)):
        a, b = own_and_other(value, who)
        own[i] = a.astype(BF)
        swap[i * tokens : (i + 1) * tokens] = b.astype(BF)
    if len(refs) > 2:
        gains_a, gains_b, recv_other = refs[:3]
        own_gain = refs[5]
        more = recv_other[2 * tokens :].astype(F32)
        total = gains_a[...] + gains_b[...] + sent[4:5] + sent[5:6] + more[4:5] + more[5:6]
        a, b = own_and_other(total, who)
        own_gain[...] = a
        swap[2 * tokens :] = stacked_rows(two_parts(b), 16, b.shape[1]).astype(BF)


def turn(who, held, own, recv, chunk, frame):
    tokens, share = own.shape[1:]
    parity = who[0] % 2
    start = pl.multiple_of(frame * chunk, chunk)
    for i in range(2):
        held[2 * i + parity] = own[i, pl.ds(start, chunk)].astype(F32)
        held[2 * i + 1 - parity] = recv[pl.ds(i * tokens + start, chunk)].astype(F32)
    return held[...].reshape(4 * chunk, share).T.astype(BF)


def pack_early_kernel(frames, slots, who, where, own, recv, *refs):
    outs, held = refs[: len(slots)], refs[len(slots)]
    chunk = own.shape[1] // frames
    for n, s in enumerate(slots):
        outs[n][...] = turn(who, held.at[n], own, recv, chunk, where[0] ^ s)


def pack_late_kernel(frames, slots, who, where, own_a, recv_a, own_b, recv_b, own_gain, *refs):
    outs, held = refs[:frames], refs[frames]
    tokens, share = own_a.shape[1:]
    chunk = tokens // frames
    lanes = outs[0].shape[1]
    sent = recv_a[2 * tokens :].astype(F32)
    value = own_gain[...] + sent[0:1] + sent[1:2]
    n_parts = -(-share // lanes)
    rows = []
    for part in two_parts(value):
        if n_parts * lanes > share:
            part = jnp.concatenate([part, jnp.zeros((1, n_parts * lanes - share), F32)], axis=1)
        rows += [part[:, i * lanes : (i + 1) * lanes] for i in range(n_parts)]
    at = outs[0].shape[0] - 2 * share
    block = stacked_rows(rows, at, lanes).astype(BF)
    for s in range(frames):
        frame = where[0] ^ s
        base = 0
        if s not in slots:
            outs[s][:share] = turn(who, held.at[s, 0], own_b, recv_b, chunk, frame)
            base = share
        outs[s][base : base + share] = turn(who, held.at[s, 1], own_a, recv_a, chunk, frame)
        outs[s][base + share :] = block


def assemble_kernel(n_slots, slots, who, where, *refs):
    soon, parts = refs[: len(slots)], refs[len(slots) : len(slots) + n_slots]
    first, second, total, held, sems = refs[len(slots) + n_slots :]
    lanes = parts[0].shape[1]
    share = first.shape[0]
    middle = lanes // 2
    low_is_late = who[0] // 2 == 0
    copies = []
    value = 0.0
    for s, part in enumerate(parts):
        if s in slots:
            other, base = soon[slots.index(s)][...], 0
        else:
            other, base = part[:share], share
        late = part[base : base + share]
        value = value + part[base + share :].astype(F32)
        low = jnp.where(low_is_late, late, other)
        high = jnp.where(low_is_late, other, late)
        held[s, 0] = jnp.concatenate([low[:, :middle], high[:, :middle]], axis=1)
        held[s, 1] = jnp.concatenate([low[:, middle:], high[:, middle:]], axis=1)
        at = pl.ds(pl.multiple_of((where[0] ^ s) * lanes, lanes), lanes)
        for i, out in enumerate((first, second)):
            copy = pltpu.make_async_copy(held.at[s, i], out.at[:, at], sems.at[2 * s + i])
            copy.start()
            copies.append(copy)
    n_parts = -(-share // lanes)
    value = value[:n_parts] + value[n_parts : 2 * n_parts]
    value = jnp.concatenate([value[i : i + 1] for i in range(n_parts)], axis=1)
    total[...] = value[:, :share]
    for copy in copies:
        copy.wait()


def call(kernel, outs, *args, scalars=1, scratch=(), in_hbm=(), out_hbm=(), limit=None):
    def space(i, hbm):
        return pl.BlockSpec(memory_space=pl.ANY if i in hbm else pltpu.VMEM)

    return pl.pallas_call(
        kernel,
        out_shape=[jax.ShapeDtypeStruct(shape, kind) for shape, kind in outs],
        in_specs=[pl.BlockSpec(memory_space=pltpu.SMEM)] * scalars
        + [space(i, in_hbm) for i in range(scalars, len(args))],
        out_specs=[space(i, out_hbm) for i in range(len(outs))],
        scratch_shapes=scratch,
        compiler_params=pltpu.CompilerParams(vmem_limit_bytes=limit or VMEM_LIMIT),
    )(*args)


EARLY = (7, 6, 5)


def block(frames_in, norm_gain, w_qkv, w_out, keep_runs, out_cotangent):
    _, place_total, width = frames_in.shape
    n_tm, n_te = lax.axis_size("tm"), lax.axis_size("tensor")
    frames = n_tm
    direct = n_tm <= 8
    n_near = n_tm // 2
    chunk = place_total // (n_tm * n_te)
    tokens = frames * chunk
    rows = 16 if chunk % 16 == 0 else chunk
    k = lax.axis_index("tm").astype(jnp.int32)
    j = lax.axis_index("tensor").astype(jnp.int32)
    where, who = k.reshape(1), j.reshape(1)
    share = w_qkv.shape[2]
    pair = 2 * share
    half = width // 2
    lanes = n_te * chunk

    gain = norm_gain

    def gather_chunks(value):
        mine = lax.dynamic_index_in_dim(
            value.reshape(n_tm, n_te, chunk, width), j, 1, keepdims=False
        )
        first = lax.all_to_all(mine, "tm", split_axis=0, concat_axis=0, tiled=True)
        return first, exchange(first, "tensor", 2)

    w_own = jnp.transpose(w_qkv, (1, 2, 0))
    w_other = exchange(w_own, "tensor", 1)
    out_other = exchange(w_out, "tensor", 1)
    if direct:
        (x_mine,) = call(
            send_x_kernel, [((n_tm, chunk, width), BF)],
            who, frames_in.reshape(n_tm, n_te, chunk, width),
            in_hbm=(1,), limit=WHOLE_VMEM,
            scratch=[pltpu.SemaphoreType.DMA((n_tm,))],
        )
        parts = call(
            functools.partial(send_c_kernel, n_near, n_tm),
            [((2, chunk, width), BF)] * n_near + [((chunk, width), BF)] * (n_tm - n_near),
            where, who, out_cotangent.reshape(n_tm, n_te, chunk, width),
            scalars=2, in_hbm=(2,), limit=WHOLE_VMEM,
            scratch=[pltpu.SemaphoreType.DMA((n_tm + n_near,))],
        )
        first = lax.all_to_all(x_mine, "tm", split_axis=0, concat_axis=0, tiled=True)
        xs = (first, exchange(first, "tensor", 2))
        far = [exchange(parts[s], "tm", s) for s in range(n_near, n_tm)]
        (local,) = call(local_kernel, [((2, chunk, width), BF)], parts[0], scalars=0)
        near = [local] + [exchange(parts[s], "tm", s) for s in range(1, n_near)]
        (stacked,) = call(
            stack_kernel, [((n_tm - n_near, chunk, width), BF)], *far,
            scalars=0,
        )
        passed = exchange(stacked, "tensor", 2)
        cs = (near + far, near + [passed] * (n_tm - n_near))
        picks = [
            [0] * n_near + [None] * (n_tm - n_near), [1] * n_near + list(range(n_tm - n_near))
        ]
    else:
        xs = gather_chunks(frames_in)
        cs = tuple([value] for value in gather_chunks(out_cotangent))
        picks = [[None], [None]]
    matrices = (w_own, w_other, w_out, out_other)

    runs = jnp.transpose(keep_runs, (0, 2, 1))
    cube = (frames, chunk)
    done, recvs = [], []
    for g in range(2):
        done.append(
            call(
                functools.partial(attend_kernel, frames, rows, picks[g], n_te, g),
                [
                    (cube + (width,), BF),
                    ((tokens, width), BF),
                    (cube + (pair,), BF),
                    (cube + (3 * pair,), BF),
                    ((2, tokens, half), F32),
                    ((2 * tokens + 16, half), BF),
                    ((2, tokens), F32),
                    ((1, half), F32),
                ],
                who, where, gain, *matrices, runs, xs[g], *cs[g],
                scalars=2,
            )
        )
        recvs.append(exchange(done[g][5], "tensor", 2))

    flat = lambda value: value.reshape(tokens, value.shape[-1])
    grad_parts = [
        call(
            functools.partial(grads_kernel, own),
            [((width, 4 * share), F32 if own else BF)],
            done[0][1], done[1][1], flat(done[0][3]), flat(done[1][3]),
            flat(done[0][0]), flat(done[1][0]), flat(done[0][2]), flat(done[1][2]),
            scalars=0,
        )[0]
        for own in (False, True)
    ]
    grad_send, grad_keep = grad_parts
    grad_recv = exchange(grad_send, "tensor", 1)
    per = width // n_tm
    bits = [1 << i for i in range(n_tm.bit_length() - 1)]
    column = 2 * share
    orders = (bits, bits[1::-1] + bits[2:])
    held = [grad_keep.reshape(n_tm, per, 4 * share)]
    moved = [grad_recv.reshape(n_tm, per, 4 * share)]
    for step in range(len(bits)):
        count = n_tm >> (step + 1)
        piece = (count, per, column)
        result = call(
            functools.partial(halve_kernel, n_tm, orders, step, len(held)),
            [(piece, F32), (piece, BF)] * 2,
            where, *held, *moved,
        )
        held = [result[0], result[2]]
        moved = [exchange(result[2 * i + 1], "tm", orders[i][step]) for i in range(2)]
    grad_qkv, grad_proj = call(
        last_grads_kernel,
        [((3, per, share), BF), ((share, per), BF)],
        *held, *moved,
        scalars=0,
    )
    grad_qkv = jnp.transpose(grad_qkv, (1, 0, 2))

    owns, swapped = [None, None], [None, None]
    for g in (1, 0):
        c_all, _, _, _, keep, _, stats, gains = done[g]
        outs = [((2, tokens, share), BF), ((2 * tokens + (0 if g else 16), share), BF)]
        more = ()
        if g == 0:
            outs.append(((1, share), F32))
            more = (gains, done[1][7], recvs[0])
        result = call(
            finish_kernel, outs,
            who, xs[g], c_all, gain, keep, recvs[1 - g], stats, *more,
        )
        owns[g], swap = result[:2]
        swapped[g] = exchange(swap, "tensor", 1)
        if g == 0:
            own_gain = result[2]

    if direct:
        n_parts = -(-share // lanes)
        extra = -(-2 * n_parts // 16) * 16
        slots = EARLY if n_tm > max(EARLY) else ()
        soon = call(
            functools.partial(pack_early_kernel, frames, slots),
            [((share, lanes), BF)] * len(slots),
            who, where, owns[1], swapped[1], scalars=2,
            scratch=[pltpu.VMEM((len(slots), n_te, chunk, share), F32)],
        ) if slots else []
        soon = [exchange(part, "tm", s) for part, s in zip(soon, slots)]
        messages = call(
            functools.partial(pack_late_kernel, frames, slots),
            [(((1 if s in slots else 2) * share + extra, lanes), BF) for s in range(frames)],
            who, where, owns[0], swapped[0], owns[1], swapped[1], own_gain,
            scalars=2,
            scratch=[pltpu.VMEM((frames, 2, n_te, chunk, share), F32)],
        )
        messages = [messages[0]] + [exchange(messages[s], "tm", s) for s in range(1, n_tm)]
        whole = ((share, place_total), BF)
        block_out, grad_in, total = call(
            functools.partial(assemble_kernel, n_tm, slots),
            [whole, whole, ((1, share), F32)], who, where, *soon, *messages,
            scalars=2, out_hbm=(0, 1),
            scratch=[
                pltpu.VMEM((n_tm, 2, share, lanes), BF), pltpu.SemaphoreType.DMA((2 * n_tm,))
            ],
        )
        block_out, grad_in = block_out.T, grad_in.T
        grad_gain = total.reshape(share)
    else:
        order = jnp.arange(n_te, dtype=jnp.int32) ^ j
        four = jnp.stack(
            [owns[0], swapped[0][: 2 * tokens].reshape(2, tokens, share),
             owns[1], swapped[1].reshape(2, tokens, share)]
        )[order].reshape(n_te, 2, frames, chunk, share)
        message = jnp.transpose(four, (2, 1, 0, 3, 4)).reshape(frames, 2, lanes, share)
        message = lax.all_to_all(message, "tm", split_axis=0, concat_axis=0, tiled=True)
        block_out = message[:, 0].reshape(place_total, share)
        grad_in = message[:, 1].reshape(place_total, share)
        sent = swapped[0][2 * tokens : 2 * tokens + 2].astype(F32)
        grad_gain = lax.psum(own_gain[0] + sent[0] + sent[1], "tm")
    return (block_out[None], grad_in[None], grad_qkv, grad_proj, grad_gain)


def solution(mesh):
    in_specs = (
        P("tm", None, None),
        P(),
        P(None, None, "tensor"),
        P("tensor", None),
        P(),
        P("tm", None, None),
    )
    out_specs = (
        P("tm", None, "tensor"),
        P("tm", None, "tensor"),
        P("tm", None, "tensor"),
        P("tensor", "tm"),
        P("tensor"),
    )
    return jax.shard_map(block, mesh=mesh, in_specs=in_specs, out_specs=out_specs, check_vma=False)
```

profile of v0, /device:TPU:0, one launch (start us, length us, event | category | flops | bytes accessed | tf_op | source)
XLA Modules:
  0.0 122.3 jit_solution(1815733046098835440)
XLA Ops:
  0.6 1.9 %shard_map.101 = bf16[8,32,768]{2,1,0:T(8,128)(2,1)} custom-call(s32[1]{0:T(128)} %bitcast.j.who, bf16[8,4,32,768]{3,2,1,0:T(8,128)(2,1)} %bitcast.41), custom_call_target="tpu_custom_call" | custom-call | tf_op jit(solution)/shard_map/pallas_call | solution.py:388
  2.5 7.5 %all-to-all-start = ((bf16[8,32,768]{2,1,0:T(8,128)(2,1)}), bf16[8,32,768]{2,1,0:T(8,128)(2,1)S(1)}, u32[]{:S(2)}, u32[]{:S(2)}) async-start(bf16[8,32,768]{2,1,0:T(8,128)(2,1)} %shard_map.101), calls=%async_computation | async-start | bytes 786432 | tf_op jit(solution)/shard_map/all_to_all | solution.py:445
  10.1 11.6 %all-to-all-done.x_in = bf16[8,32,768]{2,1,0:T(8,128)(2,1)S(1)} async-done(((bf16[8,32,768]{2,1,0:T(8,128)(2,1)}), bf16[8,32,768]{2,1,0:T(8,128)(2,1)S(1)}, u32[]{:S(2)}, u32[]{:S(2)}) %all-to-all-start) | async-done | bytes 393248 | tf_op jit(solution)/shard_map/all_to_all | solution.py:445
  23.2 1.9 %shard_map.102 = (bf16[2,32,768]{2,1,0:T(8,128)(2,1)}, bf16[2,32,768]{2,1,0:T(8,128)(2,1)}, bf16[2,32,768]{2,1,0:T(8,128)(2,1)}, bf16[2,32,768]{2,1,0:T(8,128)(2...) custom-call(s32[1]{0:T(128)} %bitcast.1.k.where, ...), custom_call_target="tpu_custom_call" | custom-call | tf_op jit(solution)/shard_map/pallas_call | solution.py:388
  26.0 3.1 %collective-permute-start.7 = (bf16[32,768]{1,0:T(8,128)(2,1)}, bf16[32,768]{1,0:T(8,128)(2,1)S(1)}, u32[]{:S(2)}, u32[]{:S(2)}) collective-permute-start(bf16[32,768]{1,0:T(8,128)(2,1)} %get-tuple-element.67), channel_id=1, source_target_pairs={{0,20},{4,16},{8,28},{12,24},{16,4},{20,0},{24,12},{28,8},{1,21},{... | collective-permute-start | bytes 147464 | tf_op jit(solution)/shard_map/ppermute | solution.py:25
  31.7 1.9 %collective-permute-done.7.refs_1_.refs_5_ = bf16[32,768]{1,0:T(8,128)(2,1)S(1)} collective-permute-done((bf16[32,768]{1,0:T(8,128)(2,1)}, bf16[32,768]{1,0:T(8,128)(2,1)S(1)}, u32[]{:S(2)}, u32[]{:S(2)}) %collective-permute-start.7) | collective-permute-done | bytes 49184 | tf_op jit(solution)/shard_map/ppermute | solution.py:25
  36.9 5.6 %collective-permute-done.9.refs_3_.refs_7_ = bf16[32,768]{1,0:T(8,128)(2,1)S(1)} collective-permute-done((bf16[32,768]{1,0:T(8,128)(2,1)}, bf16[32,768]{1,0:T(8,128)(2,1)S(1)}, u32[]{:S(2)}, u32[]{:S(2)}) %collective-permute-start.9) | collective-permute-done | bytes 49184 | tf_op jit(solution)/shard_map/ppermute | solution.py:25
  43.1 5.0 %collective-permute-done.4.refs_2_ = bf16[2,32,768]{2,1,0:T(8,128)(2,1)S(1)} collective-permute-done((bf16[2,32,768]{2,1,0:T(8,128)(2,1)}, bf16[2,32,768]{2,1,0:T(8,128)(2,1)S(1)}, u32[]{:S(2)}, u32[]{:S(2)}) %collective-permute-start.4) | collective-permute-done | bytes 98336 | tf_op jit(solution)/shard_map/ppermute | solution.py:25
  49.0 4.8 %collective-permute-done.5.refs_3_ = bf16[2,32,768]{2,1,0:T(8,128)(2,1)S(1)} collective-permute-done((bf16[2,32,768]{2,1,0:T(8,128)(2,1)}, bf16[2,32,768]{2,1,0:T(8,128)(2,1)S(1)}, u32[]{:S(2)}, u32[]{:S(2)}) %collective-permute-start.5) | collective-permute-done | bytes 98336 | tf_op jit(solution)/shard_map/ppermute | solution.py:25
  53.9 5.5 %shard_map.106 = (bf16[8,32,768]{2,1,0:T(8,128)(2,1)S(1)}, bf16[256,768]{1,0:T(8,128)(2,1)S(1)}, bf16[8,32,384]{2,1,0:T(8,128)(2,1)S(1)}, bf16[8,32,1152]{2,1,0:...) custom-call(s32[1]{0:T(128)} %bitcast.j.who, ...), custom_call_target="tpu_custom_call" | custom-call | tf_op jit(solution)/shard_map/pallas_call | solution.py:388
  59.4 5.5 %shard_map.105 = (bf16[8,32,768]{2,1,0:T(8,128)(2,1)S(1)}, bf16[256,768]{1,0:T(8,128)(2,1)S(1)}, bf16[8,32,384]{2,1,0:T(8,128)(2,1)S(1)}, bf16[8,32,1152]{2,1,0:...) custom-call(s32[1]{0:T(128)} %bitcast.j.who, ...), custom_call_target="tpu_custom_call" | custom-call | tf_op jit(solution)/shard_map/pallas_call | solution.py:388
  64.8 1.8 %shard_map.113 = bf16[768,768]{1,0:T(8,128)(2,1)S(1)} custom-call(bf16[256,768]{1,0:T(8,128)(2,1)S(1)} %get-tuple-element.98.n0, bf16[256,768]{1,0:T(8,128)(2,1)S(1)} %get-tuple-element.99.n1, bf16[256,1152]{1,0:T(8,128)(2,1)S(1)} %bitcast.30, bf16[256,1152]{1,0:T(8,128)(2,1)S(1)} %bitcast.32, bf16[256,768]{1,0:T(8,128)(2,1)S(1)} %bitcast.26, ...), custom_call_target="tpu_custom_call" | custom-call | tf_op jit(solution)/shard_map/pallas_call | solution.py:388
  71.0 8.1 %collective-permute-done.11.recv.refs_2_ = bf16[528,384]{1,0:T(8,128)(2,1)S(1)} collective-permute-done((bf16[528,384]{1,0:T(8,128)(2,1)S(1)}, bf16[528,384]{1,0:T(8,128)(2,1)S(1)}, u32[]{:S(2)}, u32[]{:S(2)}) %collective-permute-start.11) | collective-permute-done | bytes 405536 | tf_op jit(solution)/shard_map/ppermute | solution.py:25
  80.0 7.2 %collective-permute-done.16.recv = bf16[528,384]{1,0:T(8,128)(2,1)S(1)} collective-permute-done((bf16[528,384]{1,0:T(8,128)(2,1)S(1)}, bf16[528,384]{1,0:T(8,128)(2,1)S(1)}, u32[]{:S(2)}, u32[]{:S(2)}) %collective-permute-start.16) | collective-permute-done | bytes 405536 | tf_op jit(solution)/shard_map/ppermute | solution.py:25
  89.1 2.3 %collective-permute-start.13 = (bf16[192,128]{1,0:T(8,128)(2,1)S(1)}, bf16[192,128]{1,0:T(8,128)(2,1)S(1)}, u32[]{:S(2)}, u32[]{:S(2)}) collective-permute-start(bf16[192,128]{1,0:T(8,128)(2,1)S(1)} %get-tuple-element.76), channel_id=1, source_target_pairs={{0,28},{4,24},{8,20},{12,16},{16,12},{20,8},{24,4},{28,0},{1,29},{... | collective-permute-start | bytes 147464 | tf_op jit(solution)/shard_map/ppermute | solution.py:25
  91.4 2.6 %collective-permute-start.14 = (bf16[192,128]{1,0:T(8,128)(2,1)S(1)}, bf16[192,128]{1,0:T(8,128)(2,1)S(1)}, u32[]{:S(2)}, u32[]{:S(2)}) collective-permute-start(bf16[192,128]{1,0:T(8,128)(2,1)S(1)} %get-tuple-element.77), channel_id=1, source_target_pairs={{0,24},{4,28},{8,16},{12,20},{16,8},{20,12},{24,0},{28,4},{1,25},{... | collective-permute-start | bytes 147464 | tf_op jit(solution)/shard_map/ppermute | solution.py:25
  96.2 2.3 %collective-permute-start.22 = (bf16[208,128]{1,0:T(8,128)(2,1)S(1)}, bf16[208,128]{1,0:T(8,128)(2,1)S(1)}, u32[]{:S(2)}, u32[]{:S(2)}) collective-permute-start(bf16[208,128]{1,0:T(8,128)(2,1)S(1)} %get-tuple-element.93), channel_id=1, source_target_pairs={{0,20},{4,16},{8,28},{12,24},{16,4},{20,0},{24,12},{28,8},{1,21},{... | collective-permute-start | bytes 159752 | tf_op jit(solution)/shard_map/ppermute | solution.py:25
  98.5 1.9 %collective-permute-start.18 = (bf16[400,128]{1,0:T(8,128)(2,1)S(1)}, bf16[400,128]{1,0:T(8,128)(2,1)S(1)}, u32[]{:S(2)}, u32[]{:S(2)}) collective-permute-start(bf16[400,128]{1,0:T(8,128)(2,1)S(1)} %get-tuple-element.89), channel_id=1, source_target_pairs={{0,4},{4,0},{8,12},{12,8},{16,20},{20,16},{24,28},{28,24},{1,5},{5... | collective-permute-start | bytes 307208 | tf_op jit(solution)/shard_map/ppermute | solution.py:25
  101.2 1.9 %collective-permute-start.23 = (bf16[208,128]{1,0:T(8,128)(2,1)S(1)}, bf16[208,128]{1,0:T(8,128)(2,1)S(1)}, u32[]{:S(2)}, u32[]{:S(2)}) collective-permute-start(bf16[208,128]{1,0:T(8,128)(2,1)S(1)} %get-tuple-element.94), channel_id=1, source_target_pairs={{0,24},{4,28},{8,16},{12,20},{16,8},{20,12},{24,0},{28,4},{1,25},{... | collective-permute-start | bytes 159752 | tf_op jit(solution)/shard_map/ppermute | solution.py:25
  103.1 3.3 %collective-permute-start.24 = (bf16[208,128]{1,0:T(8,128)(2,1)S(1)}, bf16[208,128]{1,0:T(8,128)(2,1)S(1)}, u32[]{:S(2)}, u32[]{:S(2)}) collective-permute-start(bf16[208,128]{1,0:T(8,128)(2,1)S(1)} %get-tuple-element.95), channel_id=1, source_target_pairs={{0,28},{4,24},{8,20},{12,16},{16,12},{20,8},{24,4},{28,0},{1,29},{... | collective-permute-start | bytes 159752 | tf_op jit(solution)/shard_map/ppermute | solution.py:25
  107.6 3.1 %collective-permute-start.20 = (bf16[400,128]{1,0:T(8,128)(2,1)S(1)}, bf16[400,128]{1,0:T(8,128)(2,1)S(1)}, u32[]{:S(2)}, u32[]{:S(2)}) collective-permute-start(bf16[400,128]{1,0:T(8,128)(2,1)S(1)} %get-tuple-element.91), channel_id=1, source_target_pairs={{0,12},{4,8},{8,4},{12,0},{16,28},{20,24},{24,20},{28,16},{1,13},{... | collective-permute-start | bytes 307208 | tf_op jit(solution)/shard_map/ppermute | solution.py:25
  111.4 2.3 %collective-permute-start.30 = (bf16[1,96,384]{2,1,0:T(8,128)(2,1)S(1)}, bf16[1,96,384]{2,1,0:T(8,128)(2,1)S(1)}, u32[]{:S(2)}, u32[]{:S(2)}) collective-permute-start(bf16[1,96,384]{2,1,0:T(8,128)(2,1)S(1)} %get-tuple-element.114), channel_id=1, source_target_pairs={{0,16},{4,20},{8,24},{12,28},{16,0},{20,4},{24,8},{28,12},{1,17},{... | collective-permute-start | bytes 221192 | tf_op jit(solution)/shard_map/ppermute | solution.py:25
  114.4 2.2 %collective-permute-done.20.refs_6_ = bf16[400,128]{1,0:T(8,128)(2,1)S(1)} collective-permute-done((bf16[400,128]{1,0:T(8,128)(2,1)S(1)}, bf16[400,128]{1,0:T(8,128)(2,1)S(1)}, u32[]{:S(2)}, u32[]{:S(2)}) %collective-permute-start.20) | collective-permute-done | bytes 102432 | tf_op jit(solution)/shard_map/ppermute | solution.py:25
  116.6 3.2 %collective-permute-done.21.refs_7_ = bf16[400,128]{1,0:T(8,128)(2,1)S(1)} collective-permute-done((bf16[400,128]{1,0:T(8,128)(2,1)S(1)}, bf16[400,128]{1,0:T(8,128)(2,1)S(1)}, u32[]{:S(2)}, u32[]{:S(2)}) %collective-permute-start.21) | collective-permute-done | bytes 102432 | tf_op jit(solution)/shard_map/ppermute | solution.py:25
  (69 shorter events, 25.0 us)
Async XLA Ops:
  2.5 19.1 %all-to-all-start = ((bf16[8,32,768]{2,1,0:T(8,128)(2,1)}), bf16[8,32,768]{2,1,0:T(8,128)(2,1)S(1)}, u32[]{:S(2)}, u32[]{:S(2)}) async-start(bf16[8,32,768]{2,1,0:T(8,128)(2,1)} %shard_map.101), calls=%async_computation | async-start | bytes 786432 | tf_op jit(solution)/shard_map/all_to_all | solution.py:445
  10.0 43.8 %collective-permute-start.1 = (bf16[3,192,768]{2,1,0:T(8,128)(2,1)S(1)}, bf16[3,192,768]{2,1,0:T(8,128)(2,1)S(1)}, u32[]{:S(2)}, u32[]{:S(2)}) collective-permute-start(bf16[3,192,768]{2,1,0:T(8,128)(2,1)S(1)} %bitcast.23), channel_id=1, source_target_pairs={{0,1},{1,0},{2,3},{3,2},{4,5},{5,4},{6,7},{7,6},{8,9},{9,8},{10,11... | collective-permute-start | bytes 2654216 | tf_op jit(solution)/shard_map/ppermute | solution.py:25
  21.7 37.7 %collective-permute-start = (bf16[8,32,768]{2,1,0:T(8,128)(2,1)S(1)}, bf16[8,32,768]{2,1,0:T(8,128)(2,1)S(1)}, u32[]{:S(2)}, u32[]{:S(2)}) collective-permute-start(bf16[8,32,768]{2,1,0:T(8,128)(2,1)S(1)} %all-to-all-done.x_in), channel_id=1, source_target_pairs={{0,2},{1,3},{2,0},{3,1},{4,6},{5,7},{6,4},{7,5},{8,10},{9,11},{10,... | collective-permute-start | bytes 1179656 | tf_op jit(solution)/shard_map/ppermute | solution.py:25
  26.0 7.7 %collective-permute-start.7 = (bf16[32,768]{1,0:T(8,128)(2,1)}, bf16[32,768]{1,0:T(8,128)(2,1)S(1)}, u32[]{:S(2)}, u32[]{:S(2)}) collective-permute-start(bf16[32,768]{1,0:T(8,128)(2,1)} %get-tuple-element.67), channel_id=1, source_target_pairs={{0,20},{4,16},{8,28},{12,24},{16,4},{20,0},{24,12},{28,8},{1,21},{... | collective-permute-start | bytes 147464 | tf_op jit(solution)/shard_map/ppermute | solution.py:25
  31.7 22.1 %collective-permute-start.2 = (bf16[192,768]{1,0:T(8,128)(2,1)S(1)}, bf16[192,768]{1,0:T(8,128)(2,1)S(1)}, u32[]{:S(2)}, u32[]{:S(2)}) collective-permute-start(bf16[192,768]{1,0:T(8,128)(2,1)S(1)} %copy-done.1), channel_id=1, source_target_pairs={{0,1},{1,0},{2,3},{3,2},{4,5},{5,4},{6,7},{7,6},{8,9},{9,8},{10,11... | collective-permute-start | bytes 884744 | tf_op jit(solution)/shard_map/ppermute | solution.py:25
  33.6 8.9 %collective-permute-start.3 = (bf16[2,32,768]{2,1,0:T(8,128)(2,1)}, bf16[2,32,768]{2,1,0:T(8,128)(2,1)S(1)}, u32[]{:S(2)}, u32[]{:S(2)}) collective-permute-start(bf16[2,32,768]{2,1,0:T(8,128)(2,1)} %get-tuple-element.63), channel_id=1, source_target_pairs={{0,4},{4,0},{8,12},{12,8},{16,20},{20,16},{24,28},{28,24},{1,5},{5... | collective-permute-start | bytes 294920 | tf_op jit(solution)/shard_map/ppermute | solution.py:25
  35.1 7.3 %collective-permute-start.9 = (bf16[32,768]{1,0:T(8,128)(2,1)}, bf16[32,768]{1,0:T(8,128)(2,1)S(1)}, u32[]{:S(2)}, u32[]{:S(2)}) collective-permute-start(bf16[32,768]{1,0:T(8,128)(2,1)} %get-tuple-element.69), channel_id=1, source_target_pairs={{0,28},{4,24},{8,20},{12,16},{16,12},{20,8},{24,4},{28,0},{1,29},{... | collective-permute-start | bytes 147464 | tf_op jit(solution)/shard_map/ppermute | solution.py:25
  42.5 16.8 %collective-permute-start.10 = (bf16[4,32,768]{2,1,0:T(8,128)(2,1)S(1)}, bf16[4,32,768]{2,1,0:T(8,128)(2,1)S(1)}, u32[]{:S(2)}, u32[]{:S(2)}) collective-permute-start(bf16[4,32,768]{2,1,0:T(8,128)(2,1)S(1)} %shard_map.104), channel_id=1, source_target_pairs={{0,2},{1,3},{2,0},{3,1},{4,6},{5,7},{6,4},{7,5},{8,10},{9,11},{10,... | collective-permute-start | bytes 589832 | tf_op jit(solution)/shard_map/ppermute | solution.py:25
  66.8 12.3 %collective-permute-start.11 = (bf16[528,384]{1,0:T(8,128)(2,1)S(1)}, bf16[528,384]{1,0:T(8,128)(2,1)S(1)}, u32[]{:S(2)}, u32[]{:S(2)}) collective-permute-start(bf16[528,384]{1,0:T(8,128)(2,1)S(1)} %get-tuple-element.72), channel_id=1, source_target_pairs={{0,2},{1,3},{2,0},{3,1},{4,6},{5,7},{6,4},{7,5},{8,10},{9,11},{10,... | collective-permute-start | bytes 1216520 | tf_op jit(solution)/shard_map/ppermute | solution.py:25
  67.4 19.9 %collective-permute-start.16 = (bf16[528,384]{1,0:T(8,128)(2,1)S(1)}, bf16[528,384]{1,0:T(8,128)(2,1)S(1)}, u32[]{:S(2)}, u32[]{:S(2)}) collective-permute-start(bf16[528,384]{1,0:T(8,128)(2,1)S(1)} %get-tuple-element.81), channel_id=1, source_target_pairs={{0,2},{1,3},{2,0},{3,1},{4,6},{5,7},{6,4},{7,5},{8,10},{9,11},{10,... | collective-permute-start | bytes 1216520 | tf_op jit(solution)/shard_map/ppermute | solution.py:25
  70.3 17.8 %collective-permute-start.26 = (bf16[4,96,384]{2,1,0:T(8,128)(2,1)S(1)}, bf16[4,96,384]{2,1,0:T(8,128)(2,1)S(1)}, u32[]{:S(2)}, u32[]{:S(2)}) collective-permute-start(bf16[4,96,384]{2,1,0:T(8,128)(2,1)S(1)} %get-tuple-element.106), channel_id=1, source_target_pairs={{0,4},{4,0},{8,12},{12,8},{16,20},{20,16},{24,28},{28,24},{1,5},{5... | collective-permute-start | bytes 884744 | tf_op jit(solution)/shard_map/ppermute | solution.py:25
  70.4 17.7 %collective-permute-start.27 = (bf16[4,96,384]{2,1,0:T(8,128)(2,1)S(1)}, bf16[4,96,384]{2,1,0:T(8,128)(2,1)S(1)}, u32[]{:S(2)}, u32[]{:S(2)}) collective-permute-start(bf16[4,96,384]{2,1,0:T(8,128)(2,1)S(1)} %get-tuple-element.107), channel_id=1, source_target_pairs={{0,8},{4,12},{8,0},{12,4},{16,24},{20,28},{24,16},{28,20},{1,9},{5... | collective-permute-start | bytes 884744 | tf_op jit(solution)/shard_map/ppermute | solution.py:25
  79.9 9.0 %collective-permute-start.12 = (bf16[512,192]{1,0:T(8,128)(2,1)S(1)}, bf16[512,192]{1,0:T(8,128)(2,1)S(1)}, u32[]{:S(2)}, u32[]{:S(2)}) collective-permute-start(bf16[512,192]{1,0:T(8,128)(2,1)S(1)} %get-tuple-element.75), channel_id=1, source_target_pairs={{0,1},{1,0},{2,3},{3,2},{4,5},{5,4},{6,7},{7,6},{8,9},{9,8},{10,11... | collective-permute-start | bytes 589832 | tf_op jit(solution)/shard_map/ppermute | solution.py:25
  88.3 19.3 %collective-permute-start.28 = (bf16[2,96,384]{2,1,0:T(8,128)(2,1)S(1)}, bf16[2,96,384]{2,1,0:T(8,128)(2,1)S(1)}, u32[]{:S(2)}, u32[]{:S(2)}) collective-permute-start(bf16[2,96,384]{2,1,0:T(8,128)(2,1)S(1)} %get-tuple-element.110), channel_id=1, source_target_pairs={{0,8},{4,12},{8,0},{12,4},{16,24},{20,28},{24,16},{28,20},{1,9},{5... | collective-permute-start | bytes 442376 | tf_op jit(solution)/shard_map/ppermute | solution.py:25
  88.4 22.2 %collective-permute-start.29 = (bf16[2,96,384]{2,1,0:T(8,128)(2,1)S(1)}, bf16[2,96,384]{2,1,0:T(8,128)(2,1)S(1)}, u32[]{:S(2)}, u32[]{:S(2)}) collective-permute-start(bf16[2,96,384]{2,1,0:T(8,128)(2,1)S(1)} %get-tuple-element.111), channel_id=1, source_target_pairs={{0,4},{4,0},{8,12},{12,8},{16,20},{20,16},{24,28},{28,24},{1,5},{5... | collective-permute-start | bytes 442376 | tf_op jit(solution)/shard_map/ppermute | solution.py:25
  89.1 7.1 %collective-permute-start.13 = (bf16[192,128]{1,0:T(8,128)(2,1)S(1)}, bf16[192,128]{1,0:T(8,128)(2,1)S(1)}, u32[]{:S(2)}, u32[]{:S(2)}) collective-permute-start(bf16[192,128]{1,0:T(8,128)(2,1)S(1)} %get-tuple-element.76), channel_id=1, source_target_pairs={{0,28},{4,24},{8,20},{12,16},{16,12},{20,8},{24,4},{28,0},{1,29},{... | collective-permute-start | bytes 147464 | tf_op jit(solution)/shard_map/ppermute | solution.py:25
  91.4 7.2 %collective-permute-start.14 = (bf16[192,128]{1,0:T(8,128)(2,1)S(1)}, bf16[192,128]{1,0:T(8,128)(2,1)S(1)}, u32[]{:S(2)}, u32[]{:S(2)}) collective-permute-start(bf16[192,128]{1,0:T(8,128)(2,1)S(1)} %get-tuple-element.77), channel_id=1, source_target_pairs={{0,24},{4,28},{8,16},{12,20},{16,8},{20,12},{24,0},{28,4},{1,25},{... | collective-permute-start | bytes 147464 | tf_op jit(solution)/shard_map/ppermute | solution.py:25
  94.0 7.2 %collective-permute-start.15 = (bf16[192,128]{1,0:T(8,128)(2,1)S(1)}, bf16[192,128]{1,0:T(8,128)(2,1)S(1)}, u32[]{:S(2)}, u32[]{:S(2)}) collective-permute-start(bf16[192,128]{1,0:T(8,128)(2,1)S(1)} %get-tuple-element.78), channel_id=1, source_target_pairs={{0,20},{4,16},{8,28},{12,24},{16,4},{20,0},{24,12},{28,8},{1,21},{... | collective-permute-start | bytes 147464 | tf_op jit(solution)/shard_map/ppermute | solution.py:25
  98.5 15.2 %collective-permute-start.18 = (bf16[400,128]{1,0:T(8,128)(2,1)S(1)}, bf16[400,128]{1,0:T(8,128)(2,1)S(1)}, u32[]{:S(2)}, u32[]{:S(2)}) collective-permute-start(bf16[400,128]{1,0:T(8,128)(2,1)S(1)} %get-tuple-element.89), channel_id=1, source_target_pairs={{0,4},{4,0},{8,12},{12,8},{16,20},{20,16},{24,28},{28,24},{1,5},{5... | collective-permute-start | bytes 307208 | tf_op jit(solution)/shard_map/ppermute | solution.py:25
  103.1 8.3 %collective-permute-start.24 = (bf16[208,128]{1,0:T(8,128)(2,1)S(1)}, bf16[208,128]{1,0:T(8,128)(2,1)S(1)}, u32[]{:S(2)}, u32[]{:S(2)}) collective-permute-start(bf16[208,128]{1,0:T(8,128)(2,1)S(1)} %get-tuple-element.95), channel_id=1, source_target_pairs={{0,28},{4,24},{8,20},{12,16},{16,12},{20,8},{24,4},{28,0},{1,29},{... | collective-permute-start | bytes 159752 | tf_op jit(solution)/shard_map/ppermute | solution.py:25
  107.6 9.0 %collective-permute-start.20 = (bf16[400,128]{1,0:T(8,128)(2,1)S(1)}, bf16[400,128]{1,0:T(8,128)(2,1)S(1)}, u32[]{:S(2)}, u32[]{:S(2)}) collective-permute-start(bf16[400,128]{1,0:T(8,128)(2,1)S(1)} %get-tuple-element.91), channel_id=1, source_target_pairs={{0,12},{4,8},{8,4},{12,0},{16,28},{20,24},{24,20},{28,16},{1,13},{... | collective-permute-start | bytes 307208 | tf_op jit(solution)/shard_map/ppermute | solution.py:25
  110.6 9.1 %collective-permute-start.21 = (bf16[400,128]{1,0:T(8,128)(2,1)S(1)}, bf16[400,128]{1,0:T(8,128)(2,1)S(1)}, u32[]{:S(2)}, u32[]{:S(2)}) collective-permute-start(bf16[400,128]{1,0:T(8,128)(2,1)S(1)} %get-tuple-element.92), channel_id=1, source_target_pairs={{0,16},{4,20},{8,24},{12,28},{16,0},{20,4},{24,8},{28,12},{1,17},{... | collective-permute-start | bytes 307208 | tf_op jit(solution)/shard_map/ppermute | solution.py:25
  111.4 10.0 %collective-permute-start.30 = (bf16[1,96,384]{2,1,0:T(8,128)(2,1)S(1)}, bf16[1,96,384]{2,1,0:T(8,128)(2,1)S(1)}, u32[]{:S(2)}, u32[]{:S(2)}) collective-permute-start(bf16[1,96,384]{2,1,0:T(8,128)(2,1)S(1)} %get-tuple-element.114), channel_id=1, source_target_pairs={{0,16},{4,20},{8,24},{12,28},{16,0},{20,4},{24,8},{28,12},{1,17},{... | collective-permute-start | bytes 221192 | tf_op jit(solution)/shard_map/ppermute | solution.py:25
  113.7 7.7 %collective-permute-start.31 = (bf16[1,96,384]{2,1,0:T(8,128)(2,1)S(1)}, bf16[1,96,384]{2,1,0:T(8,128)(2,1)S(1)}, u32[]{:S(2)}, u32[]{:S(2)}) collective-permute-start(bf16[1,96,384]{2,1,0:T(8,128)(2,1)S(1)} %get-tuple-element.115), channel_id=1, source_target_pairs={{0,16},{4,20},{8,24},{12,28},{16,0},{20,4},{24,8},{28,12},{1,17},{... | collective-permute-start | bytes 221192 | tf_op jit(solution)/shard_map/ppermute | solution.py:25
  (14 other events, 195.8 us)
where the time goes:
time: 123 us; the launch traced here: 122 us
  waiting for transfers between devices  54.8 us (45%)
  starting transfers between devices  42.5 us (35%)
  Pallas kernels  23.2 us (19%)
    ppermute x32, waiting for transfers between devices, exchange(): return lax.ppermute(value, axis, [(i, i ^ bit) for i in range(size)])  43.2 us
    ppermute x32, starting transfers between devices, exchange(): return lax.ppermute(value, axis, [(i, i ^ bit) for i in range(size)])  35.1 us
    pallas_call x17, Pallas kernels, call(): pl.pallas_call(kernel, out_shape=[jax.ShapeDtypeStruct(shape, kind) for s...  23.2 us
    all_to_all x1, waiting for transfers between devices, block(): lax.all_to_all(x_mine, 'tm', split_axis=0, concat_axis=0, tiled=True)  11.6 us
    all_to_all x1, starting transfers between devices, block(): lax.all_to_all(x_mine, 'tm', split_axis=0, concat_axis=0, tiled=True)  7.45 us
  transfers between devices with their start and end apart: 33, of which 14 were waited for; matrix products, arithmetic and copies ran while one was open for 0% of the time, Pallas kernels for 11%

commit v1 on v0

--- a/solution.py
+++ b/solution.py
@@ -348,40 +348,46 @@
         outs[s][base + share :] = block
 
 
-def assemble_kernel(n_slots, slots, who, where, *refs):
-    soon, parts = refs[: len(slots)], refs[len(slots) : len(slots) + n_slots]
-    first, second, total, held, sems = refs[len(slots) + n_slots :]
+def assemble_kernel(picks, slots, continuing, who, where, *refs):
+    soon_slots = [s for s in picks if s in slots]
+    soon, refs = refs[: len(soon_slots)], refs[len(soon_slots) :]
+    parts, refs = refs[: len(picks)], refs[len(picks) :]
+    before, refs = refs[: 3 * continuing], refs[3 * continuing :]
+    first, second, total, held, sems = refs
     lanes = parts[0].shape[1]
     share = first.shape[0]
     middle = lanes // 2
     low_is_late = who[0] // 2 == 0
     copies = []
     value = 0.0
-    for s, part in enumerate(parts):
+    for n, (s, part) in enumerate(zip(picks, parts)):
         if s in slots:
-            other, base = soon[slots.index(s)][...], 0
+            other, base = soon[soon_slots.index(s)][...], 0
         else:
             other, base = part[:share], share
         late = part[base : base + share]
         value = value + part[base + share :].astype(F32)
         low = jnp.where(low_is_late, late, other)
         high = jnp.where(low_is_late, other, late)
-        held[s, 0] = jnp.concatenate([low[:, :middle], high[:, :middle]], axis=1)
-        held[s, 1] = jnp.concatenate([low[:, middle:], high[:, middle:]], axis=1)
+        held[n, 0] = jnp.concatenate([low[:, :middle], high[:, :middle]], axis=1)
+        held[n, 1] = jnp.concatenate([low[:, middle:], high[:, middle:]], axis=1)
         at = pl.ds(pl.multiple_of((where[0] ^ s) * lanes, lanes), lanes)
         for i, out in enumerate((first, second)):
-            copy = pltpu.make_async_copy(held.at[s, i], out.at[:, at], sems.at[2 * s + i])
+            copy = pltpu.make_async_copy(held.at[n, i], out.at[:, at], sems.at[2 * n + i])
             copy.start()
             copies.append(copy)
     n_parts = -(-share // lanes)
     value = value[:n_parts] + value[n_parts : 2 * n_parts]
-    value = jnp.concatenate([value[i : i + 1] for i in range(n_parts)], axis=1)
-    total[...] = value[:, :share]
+    value = jnp.concatenate([value[i : i + 1] for i in range(n_parts)], axis=1)[:, :share]
+    total[...] = value + before[2][...] if continuing else value
     for copy in copies:
         copy.wait()
 
 
-def call(kernel, outs, *args, scalars=1, scratch=(), in_hbm=(), out_hbm=(), limit=None):
+def call(
+    kernel, outs, *args, scalars=1, scratch=(), in_hbm=(), out_hbm=(), limit=None,
+    aliases=None,
+):
     def space(i, hbm):
         return pl.BlockSpec(memory_space=pl.ANY if i in hbm else pltpu.VMEM)
 
@@ -392,11 +398,13 @@
         + [space(i, in_hbm) for i in range(scalars, len(args))],
         out_specs=[space(i, out_hbm) for i in range(len(outs))],
         scratch_shapes=scratch,
+        input_output_aliases=aliases or {},
         compiler_params=pltpu.CompilerParams(vmem_limit_bytes=limit or VMEM_LIMIT),
     )(*args)
 
 
 EARLY = (7, 6, 5)
+LAST = (4, 3, 2, 1)
 
 
 def block(frames_in, norm_gain, w_qkv, w_out, keep_runs, out_cotangent):
@@ -559,14 +567,25 @@
         )
         messages = [messages[0]] + [exchange(messages[s], "tm", s) for s in range(1, n_tm)]
         whole = ((share, place_total), BF)
-        block_out, grad_in, total = call(
-            functools.partial(assemble_kernel, n_tm, slots),
-            [whole, whole, ((1, share), F32)], who, where, *soon, *messages,
-            scalars=2, out_hbm=(0, 1),
-            scratch=[
-                pltpu.VMEM((n_tm, 2, share, lanes), BF), pltpu.SemaphoreType.DMA((2 * n_tm,))
-            ],
-        )
+        early = dict(zip(slots, soon))
+        last = [s for s in (LAST if slots else ()) if s < n_tm]
+        placed = []
+        for picks in ([s for s in range(n_tm) if s not in last], last):
+            if not picks:
+                continue
+            args = [early[s] for s in picks if s in early] + [messages[s] for s in picks]
+            at = 2 + len(args)
+            placed = call(
+                functools.partial(assemble_kernel, picks, slots, bool(placed)),
+                [whole, whole, ((1, share), F32)], who, where, *args, *placed,
+                scalars=2, in_hbm=(at, at + 1), out_hbm=(0, 1),
+                aliases={at: 0, at + 1: 1} if placed else None,
+                scratch=[
+                    pltpu.VMEM((len(picks), 2, share, lanes), BF),
+                    pltpu.SemaphoreType.DMA((2 * len(picks),)),
+                ],
+            )
+        block_out, grad_in, total = placed
         block_out, grad_in = block_out.T, grad_in.T
         grad_gain = total.reshape(share)
     else:

time: 123 us -> 121 us (0.984)
  waiting for transfers between devices: 54.8 us -> 52.1 us
    ppermute x32, waiting for transfers between devices: 43.2 us -> 40.5 us  [exchange(): return lax.ppermute(value, axis, [(i, i ^ bit) for i in range(size)])]
    pallas_call x17 -> x18, Pallas kernels: 23.2 us -> 23.9 us  [call(): pl.pallas_call(kernel, out_shape=[jax.ShapeDtypeStruct(shape, kind) for s...]
  transfers between devices with their start and end apart: 33 -> 33, of which waited for: 14 -> 15; matrix products, arithmetic and copies ran while one was open for 0% -> 0% of each run, Pallas kernels for 11% -> 12%
where the time goes in v1:
time: 121 us
  waiting for transfers between devices  52.1 us (43%)
  starting transfers between devices  43.1 us (36%)
  Pallas kernels  23.9 us (20%)
    ppermute x32, waiting for transfers between devices, exchange(): return lax.ppermute(value, axis, [(i, i ^ bit) for i in range(size)])  40.5 us
    ppermute x32, starting transfers between devices, exchange(): return lax.ppermute(value, axis, [(i, i ^ bit) for i in range(size)])  35.7 us
    pallas_call x18, Pallas kernels, call(): pl.pallas_call(kernel, out_shape=[jax.ShapeDtypeStruct(shape, kind) for s...  23.9 us
    all_to_all x1, waiting for transfers between devices, block(): lax.all_to_all(x_mine, 'tm', split_axis=0, concat_axis=0, tiled=True)  11.6 us
    all_to_all x1, starting transfers between devices, block(): lax.all_to_all(x_mine, 'tm', split_axis=0, concat_axis=0, tiled=True)  7.45 us
  transfers between devices with their start and end apart: 33, of which 15 were waited for; matrix products, arithmetic and copies ran while one was open for 0% of the time, Pallas kernels for 12%

profile of v1, /device:TPU:0, one launch (start us, length us, event | category | flops | bytes accessed | tf_op | source)
XLA Modules:
  0.0 120.9 jit_solution(13891064098210856850)
XLA Ops:
  0.6 1.9 %shard_map.101 = bf16[8,32,768]{2,1,0:T(8,128)(2,1)} custom-call(s32[1]{0:T(128)} %bitcast.j.who, bf16[8,4,32,768]{3,2,1,0:T(8,128)(2,1)} %bitcast.41), custom_call_target="tpu_custom_call" | custom-call | tf_op jit(solution)/shard_map/pallas_call | solution.py:394
  2.5 7.5 %all-to-all-start = ((bf16[8,32,768]{2,1,0:T(8,128)(2,1)}), bf16[8,32,768]{2,1,0:T(8,128)(2,1)S(1)}, u32[]{:S(2)}, u32[]{:S(2)}) async-start(bf16[8,32,768]{2,1,0:T(8,128)(2,1)} %shard_map.101), calls=%async_computation | async-start | bytes 786432 | tf_op jit(solution)/shard_map/all_to_all | solution.py:453
  10.1 11.6 %all-to-all-done.x_in = bf16[8,32,768]{2,1,0:T(8,128)(2,1)S(1)} async-done(((bf16[8,32,768]{2,1,0:T(8,128)(2,1)}), bf16[8,32,768]{2,1,0:T(8,128)(2,1)S(1)}, u32[]{:S(2)}, u32[]{:S(2)}) %all-to-all-start) | async-done | bytes 393248 | tf_op jit(solution)/shard_map/all_to_all | solution.py:453
  23.2 2.0 %shard_map.102 = (bf16[2,32,768]{2,1,0:T(8,128)(2,1)}, bf16[2,32,768]{2,1,0:T(8,128)(2,1)}, bf16[2,32,768]{2,1,0:T(8,128)(2,1)}, bf16[2,32,768]{2,1,0:T(8,128)(2...) custom-call(s32[1]{0:T(128)} %bitcast.1.k.where, ...), custom_call_target="tpu_custom_call" | custom-call | tf_op jit(solution)/shard_map/pallas_call | solution.py:394
  26.0 3.1 %collective-permute-start.6 = (bf16[32,768]{1,0:T(8,128)(2,1)}, bf16[32,768]{1,0:T(8,128)(2,1)S(1)}, u32[]{:S(2)}, u32[]{:S(2)}) collective-permute-start(bf16[32,768]{1,0:T(8,128)(2,1)} %get-tuple-element.70), channel_id=1, source_target_pairs={{0,20},{4,16},{8,28},{12,24},{16,4},{20,0},{24,12},{28,8},{1,21},{... | collective-permute-start | bytes 147464 | tf_op jit(solution)/shard_map/ppermute | solution.py:25
  31.7 1.9 %collective-permute-done.6.refs_5_.refs_1_ = bf16[32,768]{1,0:T(8,128)(2,1)S(1)} collective-permute-done((bf16[32,768]{1,0:T(8,128)(2,1)}, bf16[32,768]{1,0:T(8,128)(2,1)S(1)}, u32[]{:S(2)}, u32[]{:S(2)}) %collective-permute-start.6) | collective-permute-done | bytes 49184 | tf_op jit(solution)/shard_map/ppermute | solution.py:25
  35.1 1.7 %collective-permute-start.8 = (bf16[32,768]{1,0:T(8,128)(2,1)}, bf16[32,768]{1,0:T(8,128)(2,1)S(1)}, u32[]{:S(2)}, u32[]{:S(2)}) collective-permute-start(bf16[32,768]{1,0:T(8,128)(2,1)} %get-tuple-element.72), channel_id=1, source_target_pairs={{0,28},{4,24},{8,20},{12,16},{16,12},{20,8},{24,4},{28,0},{1,29},{... | collective-permute-start | bytes 147464 | tf_op jit(solution)/shard_map/ppermute | solution.py:25
  36.9 5.6 %collective-permute-done.8.refs_7_.refs_3_ = bf16[32,768]{1,0:T(8,128)(2,1)S(1)} collective-permute-done((bf16[32,768]{1,0:T(8,128)(2,1)}, bf16[32,768]{1,0:T(8,128)(2,1)S(1)}, u32[]{:S(2)}, u32[]{:S(2)}) %collective-permute-start.8) | collective-permute-done | bytes 49184 | tf_op jit(solution)/shard_map/ppermute | solution.py:25
  43.1 5.0 %collective-permute-done.3.refs_2_ = bf16[2,32,768]{2,1,0:T(8,128)(2,1)S(1)} collective-permute-done((bf16[2,32,768]{2,1,0:T(8,128)(2,1)}, bf16[2,32,768]{2,1,0:T(8,128)(2,1)S(1)}, u32[]{:S(2)}, u32[]{:S(2)}) %collective-permute-start.3) | collective-permute-done | bytes 98336 | tf_op jit(solution)/shard_map/ppermute | solution.py:25
  49.0 4.8 %collective-permute-done.4.refs_3_ = bf16[2,32,768]{2,1,0:T(8,128)(2,1)S(1)} collective-permute-done((bf16[2,32,768]{2,1,0:T(8,128)(2,1)}, bf16[2,32,768]{2,1,0:T(8,128)(2,1)S(1)}, u32[]{:S(2)}, u32[]{:S(2)}) %collective-permute-start.4) | collective-permute-done | bytes 98336 | tf_op jit(solution)/shard_map/ppermute | solution.py:25
  53.9 5.5 %shard_map.104 = (bf16[8,32,768]{2,1,0:T(8,128)(2,1)S(1)}, bf16[256,768]{1,0:T(8,128)(2,1)S(1)}, bf16[8,32,384]{2,1,0:T(8,128)(2,1)S(1)}, bf16[8,32,1152]{2,1,0:...) custom-call(s32[1]{0:T(128)} %bitcast.j.who, ...), custom_call_target="tpu_custom_call" | custom-call | tf_op jit(solution)/shard_map/pallas_call | solution.py:394
  59.4 5.5 %shard_map.106 = (bf16[8,32,768]{2,1,0:T(8,128)(2,1)S(1)}, bf16[256,768]{1,0:T(8,128)(2,1)S(1)}, bf16[8,32,384]{2,1,0:T(8,128)(2,1)S(1)}, bf16[8,32,1152]{2,1,0:...) custom-call(s32[1]{0:T(128)} %bitcast.j.who, ...), custom_call_target="tpu_custom_call" | custom-call | tf_op jit(solution)/shard_map/pallas_call | solution.py:394
  64.8 1.8 %shard_map.114 = bf16[768,768]{1,0:T(8,128)(2,1)S(1)} custom-call(bf16[256,768]{1,0:T(8,128)(2,1)S(1)} %get-tuple-element.104.n0, bf16[256,768]{1,0:T(8,128)(2,1)S(1)} %get-tuple-element.105.n1, bf16[256,1152]{1,0:T(8,128)(2,1)S(1)} %bitcast.30, bf16[256,1152]{1,0:T(8,128)(2,1)S(1)} %bitcast.32, bf16[256,768]{1,0:T(8,128)(2,1)S(1)} %bitcast.26, ...), custom_call_target="tpu_custom_call" | custom-call | tf_op jit(solution)/shard_map/pallas_call | solution.py:394
  67.4 1.5 %collective-permute-start.11 = (bf16[528,384]{1,0:T(8,128)(2,1)S(1)}, bf16[528,384]{1,0:T(8,128)(2,1)S(1)}, u32[]{:S(2)}, u32[]{:S(2)}) collective-permute-start(bf16[528,384]{1,0:T(8,128)(2,1)S(1)} %get-tuple-element.75), channel_id=1, source_target_pairs={{0,2},{1,3},{2,0},{3,1},{4,6},{5,7},{6,4},{7,5},{8,10},{9,11},{10,... | collective-permute-start | bytes 1216520 | tf_op jit(solution)/shard_map/ppermute | solution.py:25
  71.0 8.1 %collective-permute-done.12.refs_2_.recv = bf16[528,384]{1,0:T(8,128)(2,1)S(1)} collective-permute-done((bf16[528,384]{1,0:T(8,128)(2,1)S(1)}, bf16[528,384]{1,0:T(8,128)(2,1)S(1)}, u32[]{:S(2)}, u32[]{:S(2)}) %collective-permute-start.12) | collective-permute-done | bytes 405536 | tf_op jit(solution)/shard_map/ppermute | solution.py:25
  80.0 7.2 %collective-permute-done.11.recv = bf16[528,384]{1,0:T(8,128)(2,1)S(1)} collective-permute-done((bf16[528,384]{1,0:T(8,128)(2,1)S(1)}, bf16[528,384]{1,0:T(8,128)(2,1)S(1)}, u32[]{:S(2)}, u32[]{:S(2)}) %collective-permute-start.11) | collective-permute-done | bytes 405536 | tf_op jit(solution)/shard_map/ppermute | solution.py:25
  89.1 2.8 %collective-permute-start.19 = (bf16[192,128]{1,0:T(8,128)(2,1)S(1)}, bf16[192,128]{1,0:T(8,128)(2,1)S(1)}, u32[]{:S(2)}, u32[]{:S(2)}) collective-permute-start(bf16[192,128]{1,0:T(8,128)(2,1)S(1)} %get-tuple-element.92), channel_id=1, source_target_pairs={{0,20},{4,16},{8,28},{12,24},{16,4},{20,0},{24,12},{28,8},{1,21},{... | collective-permute-start | bytes 147464 | tf_op jit(solution)/shard_map/ppermute | solution.py:25
  91.9 2.6 %collective-permute-start.20 = (bf16[192,128]{1,0:T(8,128)(2,1)S(1)}, bf16[192,128]{1,0:T(8,128)(2,1)S(1)}, u32[]{:S(2)}, u32[]{:S(2)}) collective-permute-start(bf16[192,128]{1,0:T(8,128)(2,1)S(1)} %get-tuple-element.93), channel_id=1, source_target_pairs={{0,24},{4,28},{8,16},{12,20},{16,8},{20,12},{24,0},{28,4},{1,25},{... | collective-permute-start | bytes 147464 | tf_op jit(solution)/shard_map/ppermute | solution.py:25
  97.9 3.8 %collective-permute-start.15 = (bf16[400,128]{1,0:T(8,128)(2,1)S(1)}, bf16[400,128]{1,0:T(8,128)(2,1)S(1)}, u32[]{:S(2)}, u32[]{:S(2)}) collective-permute-start(bf16[400,128]{1,0:T(8,128)(2,1)S(1)} %get-tuple-element.88), channel_id=1, source_target_pairs={{0,16},{4,20},{8,24},{12,28},{16,0},{20,4},{24,8},{28,12},{1,17},{... | collective-permute-start | bytes 307208 | tf_op jit(solution)/shard_map/ppermute | solution.py:25
  102.8 3.1 %collective-permute-done.22.refs_4_ = bf16[208,128]{1,0:T(8,128)(2,1)S(1)} collective-permute-done((bf16[208,128]{1,0:T(8,128)(2,1)S(1)}, bf16[208,128]{1,0:T(8,128)(2,1)S(1)}, u32[]{:S(2)}, u32[]{:S(2)}) %collective-permute-start.22) | collective-permute-done | bytes 53280 | tf_op jit(solution)/shard_map/ppermute | solution.py:25
  105.9 1.7 %collective-permute-start.24 = (bf16[208,128]{1,0:T(8,128)(2,1)S(1)}, bf16[208,128]{1,0:T(8,128)(2,1)S(1)}, u32[]{:S(2)}, u32[]{:S(2)}) collective-permute-start(bf16[208,128]{1,0:T(8,128)(2,1)S(1)} %get-tuple-element.98), channel_id=1, source_target_pairs={{0,28},{4,24},{8,20},{12,16},{16,12},{20,8},{24,4},{28,0},{1,29},{... | collective-permute-start | bytes 159752 | tf_op jit(solution)/shard_map/ppermute | solution.py:25
  107.7 3.3 %collective-permute-start.16 = (bf16[400,128]{1,0:T(8,128)(2,1)S(1)}, bf16[400,128]{1,0:T(8,128)(2,1)S(1)}, u32[]{:S(2)}, u32[]{:S(2)}) collective-permute-start(bf16[400,128]{1,0:T(8,128)(2,1)S(1)} %get-tuple-element.89), channel_id=1, source_target_pairs={{0,12},{4,8},{8,4},{12,0},{16,28},{20,24},{24,20},{28,16},{1,13},{... | collective-permute-start | bytes 307208 | tf_op jit(solution)/shard_map/ppermute | solution.py:25
  113.1 1.8 %collective-permute-start.30 = (bf16[1,96,384]{2,1,0:T(8,128)(2,1)S(1)}, bf16[1,96,384]{2,1,0:T(8,128)(2,1)S(1)}, u32[]{:S(2)}, u32[]{:S(2)}) collective-permute-start(bf16[1,96,384]{2,1,0:T(8,128)(2,1)S(1)} %get-tuple-element.120), channel_id=1, source_target_pairs={{0,16},{4,20},{8,24},{12,28},{16,0},{20,4},{24,8},{28,12},{1,17},{... | collective-permute-start | bytes 221192 | tf_op jit(solution)/shard_map/ppermute | solution.py:25
  116.9 1.7 %collective-permute-done.17.refs_2_ = bf16[400,128]{1,0:T(8,128)(2,1)S(1)} collective-permute-done((bf16[400,128]{1,0:T(8,128)(2,1)S(1)}, bf16[400,128]{1,0:T(8,128)(2,1)S(1)}, u32[]{:S(2)}, u32[]{:S(2)}) %collective-permute-start.17) | collective-permute-done | bytes 102432 | tf_op jit(solution)/shard_map/ppermute | solution.py:25
  (70 shorter events, 24.8 us)
Async XLA Ops:
  2.5 19.1 %all-to-all-start = ((bf16[8,32,768]{2,1,0:T(8,128)(2,1)}), bf16[8,32,768]{2,1,0:T(8,128)(2,1)S(1)}, u32[]{:S(2)}, u32[]{:S(2)}) async-start(bf16[8,32,768]{2,1,0:T(8,128)(2,1)} %shard_map.101), calls=%async_computation | async-start | bytes 786432 | tf_op jit(solution)/shard_map/all_to_all | solution.py:453
  10.0 43.9 %collective-permute-start = (bf16[3,192,768]{2,1,0:T(8,128)(2,1)S(1)}, bf16[3,192,768]{2,1,0:T(8,128)(2,1)S(1)}, u32[]{:S(2)}, u32[]{:S(2)}) collective-permute-start(bf16[3,192,768]{2,1,0:T(8,128)(2,1)S(1)} %bitcast.23), channel_id=1, source_target_pairs={{0,1},{1,0},{2,3},{3,2},{4,5},{5,4},{6,7},{7,6},{8,9},{9,8},{10,11... | collective-permute-start | bytes 2654216 | tf_op jit(solution)/shard_map/ppermute | solution.py:25
  21.7 37.7 %collective-permute-start.9 = (bf16[8,32,768]{2,1,0:T(8,128)(2,1)S(1)}, bf16[8,32,768]{2,1,0:T(8,128)(2,1)S(1)}, u32[]{:S(2)}, u32[]{:S(2)}) collective-permute-start(bf16[8,32,768]{2,1,0:T(8,128)(2,1)S(1)} %all-to-all-done.x_in), channel_id=1, source_target_pairs={{0,2},{1,3},{2,0},{3,1},{4,6},{5,7},{6,4},{7,5},{8,10},{9,11},{10,... | collective-permute-start | bytes 1179656 | tf_op jit(solution)/shard_map/ppermute | solution.py:25
  26.0 7.7 %collective-permute-start.6 = (bf16[32,768]{1,0:T(8,128)(2,1)}, bf16[32,768]{1,0:T(8,128)(2,1)S(1)}, u32[]{:S(2)}, u32[]{:S(2)}) collective-permute-start(bf16[32,768]{1,0:T(8,128)(2,1)} %get-tuple-element.70), channel_id=1, source_target_pairs={{0,20},{4,16},{8,28},{12,24},{16,4},{20,0},{24,12},{28,8},{1,21},{... | collective-permute-start | bytes 147464 | tf_op jit(solution)/shard_map/ppermute | solution.py:25
  31.7 22.1 %collective-permute-start.1 = (bf16[192,768]{1,0:T(8,128)(2,1)S(1)}, bf16[192,768]{1,0:T(8,128)(2,1)S(1)}, u32[]{:S(2)}, u32[]{:S(2)}) collective-permute-start(bf16[192,768]{1,0:T(8,128)(2,1)S(1)} %copy-done.1), channel_id=1, source_target_pairs={{0,1},{1,0},{2,3},{3,2},{4,5},{5,4},{6,7},{7,6},{8,9},{9,8},{10,11... | collective-permute-start | bytes 884744 | tf_op jit(solution)/shard_map/ppermute | solution.py:25
  33.6 8.9 %collective-permute-start.2 = (bf16[2,32,768]{2,1,0:T(8,128)(2,1)}, bf16[2,32,768]{2,1,0:T(8,128)(2,1)S(1)}, u32[]{:S(2)}, u32[]{:S(2)}) collective-permute-start(bf16[2,32,768]{2,1,0:T(8,128)(2,1)} %get-tuple-element.66), channel_id=1, source_target_pairs={{0,4},{4,0},{8,12},{12,8},{16,20},{20,16},{24,28},{28,24},{1,5},{5... | collective-permute-start | bytes 294920 | tf_op jit(solution)/shard_map/ppermute | solution.py:25
  35.1 7.3 %collective-permute-start.8 = (bf16[32,768]{1,0:T(8,128)(2,1)}, bf16[32,768]{1,0:T(8,128)(2,1)S(1)}, u32[]{:S(2)}, u32[]{:S(2)}) collective-permute-start(bf16[32,768]{1,0:T(8,128)(2,1)} %get-tuple-element.72), channel_id=1, source_target_pairs={{0,28},{4,24},{8,20},{12,16},{16,12},{20,8},{24,4},{28,0},{1,29},{... | collective-permute-start | bytes 147464 | tf_op jit(solution)/shard_map/ppermute | solution.py:25
  42.5 16.8 %collective-permute-start.10 = (bf16[4,32,768]{2,1,0:T(8,128)(2,1)S(1)}, bf16[4,32,768]{2,1,0:T(8,128)(2,1)S(1)}, u32[]{:S(2)}, u32[]{:S(2)}) collective-permute-start(bf16[4,32,768]{2,1,0:T(8,128)(2,1)S(1)} %shard_map.105), channel_id=1, source_target_pairs={{0,2},{1,3},{2,0},{3,1},{4,6},{5,7},{6,4},{7,5},{8,10},{9,11},{10,... | collective-permute-start | bytes 589832 | tf_op jit(solution)/shard_map/ppermute | solution.py:25
  66.8 12.3 %collective-permute-start.12 = (bf16[528,384]{1,0:T(8,128)(2,1)S(1)}, bf16[528,384]{1,0:T(8,128)(2,1)S(1)}, u32[]{:S(2)}, u32[]{:S(2)}) collective-permute-start(bf16[528,384]{1,0:T(8,128)(2,1)S(1)} %get-tuple-element.79), channel_id=1, source_target_pairs={{0,2},{1,3},{2,0},{3,1},{4,6},{5,7},{6,4},{7,5},{8,10},{9,11},{10,... | collective-permute-start | bytes 1216520 | tf_op jit(solution)/shard_map/ppermute | solution.py:25
  67.4 19.9 %collective-permute-start.11 = (bf16[528,384]{1,0:T(8,128)(2,1)S(1)}, bf16[528,384]{1,0:T(8,128)(2,1)S(1)}, u32[]{:S(2)}, u32[]{:S(2)}) collective-permute-start(bf16[528,384]{1,0:T(8,128)(2,1)S(1)} %get-tuple-element.75), channel_id=1, source_target_pairs={{0,2},{1,3},{2,0},{3,1},{4,6},{5,7},{6,4},{7,5},{8,10},{9,11},{10,... | collective-permute-start | bytes 1216520 | tf_op jit(solution)/shard_map/ppermute | solution.py:25
  70.4 17.8 %collective-permute-start.26 = (bf16[4,96,384]{2,1,0:T(8,128)(2,1)S(1)}, bf16[4,96,384]{2,1,0:T(8,128)(2,1)S(1)}, u32[]{:S(2)}, u32[]{:S(2)}) collective-permute-start(bf16[4,96,384]{2,1,0:T(8,128)(2,1)S(1)} %get-tuple-element.112), channel_id=1, source_target_pairs={{0,4},{4,0},{8,12},{12,8},{16,20},{20,16},{24,28},{28,24},{1,5},{5... | collective-permute-start | bytes 884744 | tf_op jit(solution)/shard_map/ppermute | solution.py:25
  70.4 17.8 %collective-permute-start.27 = (bf16[4,96,384]{2,1,0:T(8,128)(2,1)S(1)}, bf16[4,96,384]{2,1,0:T(8,128)(2,1)S(1)}, u32[]{:S(2)}, u32[]{:S(2)}) collective-permute-start(bf16[4,96,384]{2,1,0:T(8,128)(2,1)S(1)} %get-tuple-element.113), channel_id=1, source_target_pairs={{0,8},{4,12},{8,0},{12,4},{16,24},{20,28},{24,16},{28,20},{1,9},{5... | collective-permute-start | bytes 884744 | tf_op jit(solution)/shard_map/ppermute | solution.py:25
  79.9 9.0 %collective-permute-start.14 = (bf16[512,192]{1,0:T(8,128)(2,1)S(1)}, bf16[512,192]{1,0:T(8,128)(2,1)S(1)}, u32[]{:S(2)}, u32[]{:S(2)}) collective-permute-start(bf16[512,192]{1,0:T(8,128)(2,1)S(1)} %get-tuple-element.86), channel_id=1, source_target_pairs={{0,1},{1,0},{2,3},{3,2},{4,5},{5,4},{6,7},{7,6},{8,9},{9,8},{10,11... | collective-permute-start | bytes 589832 | tf_op jit(solution)/shard_map/ppermute | solution.py:25
  88.3 22.7 %collective-permute-start.28 = (bf16[2,96,384]{2,1,0:T(8,128)(2,1)S(1)}, bf16[2,96,384]{2,1,0:T(8,128)(2,1)S(1)}, u32[]{:S(2)}, u32[]{:S(2)}) collective-permute-start(bf16[2,96,384]{2,1,0:T(8,128)(2,1)S(1)} %get-tuple-element.116), channel_id=1, source_target_pairs={{0,8},{4,12},{8,0},{12,4},{16,24},{20,28},{24,16},{28,20},{1,9},{5... | collective-permute-start | bytes 442376 | tf_op jit(solution)/shard_map/ppermute | solution.py:25
  88.5 22.5 %collective-permute-start.29 = (bf16[2,96,384]{2,1,0:T(8,128)(2,1)S(1)}, bf16[2,96,384]{2,1,0:T(8,128)(2,1)S(1)}, u32[]{:S(2)}, u32[]{:S(2)}) collective-permute-start(bf16[2,96,384]{2,1,0:T(8,128)(2,1)S(1)} %get-tuple-element.117), channel_id=1, source_target_pairs={{0,4},{4,0},{8,12},{12,8},{16,20},{20,16},{24,28},{28,24},{1,5},{5... | collective-permute-start | bytes 442376 | tf_op jit(solution)/shard_map/ppermute | solution.py:25
  89.1 7.9 %collective-permute-start.19 = (bf16[192,128]{1,0:T(8,128)(2,1)S(1)}, bf16[192,128]{1,0:T(8,128)(2,1)S(1)}, u32[]{:S(2)}, u32[]{:S(2)}) collective-permute-start(bf16[192,128]{1,0:T(8,128)(2,1)S(1)} %get-tuple-element.92), channel_id=1, source_target_pairs={{0,20},{4,16},{8,28},{12,24},{16,4},{20,0},{24,12},{28,8},{1,21},{... | collective-permute-start | bytes 147464 | tf_op jit(solution)/shard_map/ppermute | solution.py:25
  94.5 7.2 %collective-permute-start.21 = (bf16[192,128]{1,0:T(8,128)(2,1)S(1)}, bf16[192,128]{1,0:T(8,128)(2,1)S(1)}, u32[]{:S(2)}, u32[]{:S(2)}) collective-permute-start(bf16[192,128]{1,0:T(8,128)(2,1)S(1)} %get-tuple-element.94), channel_id=1, source_target_pairs={{0,28},{4,24},{8,20},{12,16},{16,12},{20,8},{24,4},{28,0},{1,29},{... | collective-permute-start | bytes 147464 | tf_op jit(solution)/shard_map/ppermute | solution.py:25
  97.0 8.9 %collective-permute-start.22 = (bf16[208,128]{1,0:T(8,128)(2,1)S(1)}, bf16[208,128]{1,0:T(8,128)(2,1)S(1)}, u32[]{:S(2)}, u32[]{:S(2)}) collective-permute-start(bf16[208,128]{1,0:T(8,128)(2,1)S(1)} %get-tuple-element.96), channel_id=1, source_target_pairs={{0,20},{4,16},{8,28},{12,24},{16,4},{20,0},{24,12},{28,8},{1,21},{... | collective-permute-start | bytes 159752 | tf_op jit(solution)/shard_map/ppermute | solution.py:25
  97.9 17.0 %collective-permute-start.15 = (bf16[400,128]{1,0:T(8,128)(2,1)S(1)}, bf16[400,128]{1,0:T(8,128)(2,1)S(1)}, u32[]{:S(2)}, u32[]{:S(2)}) collective-permute-start(bf16[400,128]{1,0:T(8,128)(2,1)S(1)} %get-tuple-element.88), channel_id=1, source_target_pairs={{0,16},{4,20},{8,24},{12,28},{16,0},{20,4},{24,8},{28,12},{1,17},{... | collective-permute-start | bytes 307208 | tf_op jit(solution)/shard_map/ppermute | solution.py:25
  105.9 7.1 %collective-permute-start.24 = (bf16[208,128]{1,0:T(8,128)(2,1)S(1)}, bf16[208,128]{1,0:T(8,128)(2,1)S(1)}, u32[]{:S(2)}, u32[]{:S(2)}) collective-permute-start(bf16[208,128]{1,0:T(8,128)(2,1)S(1)} %get-tuple-element.98), channel_id=1, source_target_pairs={{0,28},{4,24},{8,20},{12,16},{16,12},{20,8},{24,4},{28,0},{1,29},{... | collective-permute-start | bytes 159752 | tf_op jit(solution)/shard_map/ppermute | solution.py:25
  107.7 9.2 %collective-permute-start.16 = (bf16[400,128]{1,0:T(8,128)(2,1)S(1)}, bf16[400,128]{1,0:T(8,128)(2,1)S(1)}, u32[]{:S(2)}, u32[]{:S(2)}) collective-permute-start(bf16[400,128]{1,0:T(8,128)(2,1)S(1)} %get-tuple-element.89), channel_id=1, source_target_pairs={{0,12},{4,8},{8,4},{12,0},{16,28},{20,24},{24,20},{28,16},{1,13},{... | collective-permute-start | bytes 307208 | tf_op jit(solution)/shard_map/ppermute | solution.py:25
  111.0 7.6 %collective-permute-start.17 = (bf16[400,128]{1,0:T(8,128)(2,1)S(1)}, bf16[400,128]{1,0:T(8,128)(2,1)S(1)}, u32[]{:S(2)}, u32[]{:S(2)}) collective-permute-start(bf16[400,128]{1,0:T(8,128)(2,1)S(1)} %get-tuple-element.90), channel_id=1, source_target_pairs={{0,8},{4,12},{8,0},{12,4},{16,24},{20,28},{24,16},{28,20},{1,9},{5... | collective-permute-start | bytes 307208 | tf_op jit(solution)/shard_map/ppermute | solution.py:25
  111.0 7.6 %collective-permute-start.18 = (bf16[400,128]{1,0:T(8,128)(2,1)S(1)}, bf16[400,128]{1,0:T(8,128)(2,1)S(1)}, u32[]{:S(2)}, u32[]{:S(2)}) collective-permute-start(bf16[400,128]{1,0:T(8,128)(2,1)S(1)} %get-tuple-element.91), channel_id=1, source_target_pairs={{0,4},{4,0},{8,12},{12,8},{16,20},{20,16},{24,28},{28,24},{1,5},{5... | collective-permute-start | bytes 307208 | tf_op jit(solution)/shard_map/ppermute | solution.py:25
  113.1 7.0 %collective-permute-start.30 = (bf16[1,96,384]{2,1,0:T(8,128)(2,1)S(1)}, bf16[1,96,384]{2,1,0:T(8,128)(2,1)S(1)}, u32[]{:S(2)}, u32[]{:S(2)}) collective-permute-start(bf16[1,96,384]{2,1,0:T(8,128)(2,1)S(1)} %get-tuple-element.120), channel_id=1, source_target_pairs={{0,16},{4,20},{8,24},{12,28},{16,0},{20,4},{24,8},{28,12},{1,17},{... | collective-permute-start | bytes 221192 | tf_op jit(solution)/shard_map/ppermute | solution.py:25
  (14 other events, 193.3 us)
